TPU v7x, 32 devices: a whole 2x2x4 slice. The times are simulated.
32 devices in a mesh: row: 4 (over y, core), col: 8 (over z, x).
Axes of the slice: x: 2, y: 2, z: 4, core: 2. Of those that a mesh axis runs over, the one named last changes fastest.
Arguments:
- integrals: bfloat16 [4, 8, 32, 512, 512], P('row', 'col'), may hold values from -0.0625 to 0.0625
- tile_count: int32 [4, 8], P('row', 'col'), may hold values from 1 to 32, as said below
- tile_list: int32 [4, 8, 32], P('row', 'col'), may hold values from 0 to 31, as said below
- amplitudes: bfloat16 [32, 512, 1024], P('col', 'row'), may hold values from -6 to 6
- pair_energy: float32 [16384], P(('row', 'col')), may hold values from 1 to 4
- occ_energy: float32 [32], replicated, may hold values from -1.5 to -0.25
- partner: int32 [16384], P(('row', 'col')), may hold values from 0 to 16383, as said below
Outputs:
- amp_update: float32 [16384, 1024], P(('row', 'col'))
Inputs may be any that keep to these rules, and one draw needn't show every extreme that they name: `tile_count`: some grid cell holds exactly 32 live tiles. `tile_list`: each grid cell's list is a permutation of 0 to 31; only its first tile_count entries name live tiles. partner is an involution. Numbering the rows in consecutive blocks of 512, the rows of one block have their partners among the 8 blocks of the same aligned group of 4096 rows, exactly 64 of them in each of these blocks.
All inputs are finite; a program needn't handle non-finite values.
Results may differ from a plain program's by a relative error of at most 0.0003.
Values may be sent and summed in bfloat16 or wider, within the bound.
A program may use at most 128 MiB of HBM per device.

v0:
```python
import functools

import jax
import jax.numpy as jnp
from jax import lax
from jax.experimental import pallas as pl
from jax.experimental.pallas import tpu as pltpu
from jax.sharding import PartitionSpec as P

MESH = pl.DeviceIdType.MESH
F32, BF16, I32, I16 = jnp.float32, jnp.bfloat16, jnp.int32, jnp.int16
LEVELS = 32767.0


def iota(shape, axis):
    return lax.broadcasted_iota(I32, shape, axis)


def row_places(partner, me, n):
    rows = partner.shape[0]
    half = rows // n // 2
    own = (n + 1) * half
    local = partner % (n * rows)
    block, within = local // rows, local % rows
    index = jnp.arange(rows, dtype=I32)
    key = jnp.where(block < me, within, index)
    before = (block[None, :] == block[:, None]) & (key[None, :] < key[:, None])
    rank = jnp.sum(before.astype(I32), axis=1)
    shift = (block - me + n) % n
    owned = jnp.where(me < block, rank < half, rank >= half)
    step = (shift - 1) * half + rank % half
    place = jnp.where(block == me, rank, jnp.where(owned, 2 * half + step, own + step))
    found = jnp.sum(jnp.where(index[None, :] == within[:, None], place[None, :], 0), axis=1)
    mirror = jnp.where(block == me, rows + found, -1)
    return place, mirror


def gather_kernel(n, mine_ref, all_ref, landed, send_sem, recv_sem):
    me = lax.axis_index("col")
    barrier = pltpu.get_barrier_semaphore()
    for d in range(1, n):
        pl.semaphore_signal(barrier, inc=1, device_id={"col": lax.rem(me + d, n)}, device_id_type=MESH)
    pl.semaphore_wait(barrier, n - 1)

    def copy(d):
        return pltpu.make_async_remote_copy(
            src_ref=mine_ref, dst_ref=landed.at[d], send_sem=send_sem.at[d], recv_sem=recv_sem.at[d],
            device_id={"col": lax.rem(me + d, n)}, device_id_type=MESH,
        )

    for d in range(1, n):
        copy(d).start()
    all_ref[me] = mine_ref[...]
    for d in range(1, n):
        copy(d).wait_recv()
        all_ref[lax.rem(me + n - d, n)] = landed[d]
    for d in range(1, n):
        copy(d).wait_send()


def sort_kernel(n, half, occ, bc, slot_ref, count_ref, *refs):
    tiles, (place_ref, u_ref, w_ref, swap_ref) = refs[:bc], refs[bc:]
    i = pl.program_id(0)
    rows = place_ref.shape[2]
    tile = tiles[0].shape[3]
    own = (n + 1) * half

    total = swap_ref.shape[1]
    chunk = swap_ref.shape[0]
    x = iota((chunk, total), 0) + i * chunk
    y = iota((chunk, total), 1)
    swap_ref[...] = (x == (y % occ) * occ + y // occ).astype(F32).astype(BF16)

    for j in range(tile // rows):
        o = i * (tile // rows) + j
        equal = iota((rows, rows), 0) == place_ref[o]
        for c in range(bc):
            hit = equal & (slot_ref[i * bc + c] < count_ref[0])
            one_hot = hit.astype(F32).astype(BF16)
            got = jnp.dot(one_hot, tiles[c][0, 0, 0, j * rows : (j + 1) * rows, :], preferred_element_type=F32)
            at = slice(c * tile, (c + 1) * tile)
            u_ref[j, :, at] = got[:own].astype(BF16)
            for d in range(1, n):
                a = lax.rem(o + d, n)
                start = (n - d - 1) * half
                w_ref[a, start : start + half, at] = got[own + (d - 1) * half : own + d * half].astype(BF16)


def reduce_kernel(
    n, half, ranks, wide, u_hbm, w_hbm, swap_hbm, *refs
):
    held = ranks // 2 + 1
    given, refs = refs[:held], refs[held:]
    pieces = [given[0], given[1]]
    for piece in given[2:]:
        pieces += [piece, None]
    (
        z_ref, ubuf, wbuf, tall, t2buf, swap, sbuf, q1s, s1s, q1r, s1r, q2s, s2s, q2r, s2r, xqs, xss, xqr, xsr,
        usem, wsem, tsem, psem, q1a, q1b, s1a, s1b, q2a, q2b, s2a, s2b, xqa, xqb, xsa, xsb, psend, precv,
    ) = refs
    me = lax.axis_index("col")
    row = lax.axis_index("row")
    levels = n // 2
    level, side = me // 2, lax.rem(me, 2)
    other = me + 1 - 2 * side
    bc, tile, width = tall.shape
    depth = bc * tile
    share = tile // ranks
    own = (n + 1) * half
    chunks = n + 1

    def load_t(k):
        source = lax.rem(row + 2 * (k // 2), ranks)
        source = source if k % 2 == 0 else source + 1 - 2 * lax.rem(source, 2)
        first = pl.multiple_of(source * share, share)
        return pltpu.make_async_copy(pieces[k], tall.at[:, pl.ds(first, share), :], tsem.at[k])

    def swap_t(k):
        first = pl.multiple_of(lax.rem(row + 2 * (k // 2), ranks) * share, share)
        return pltpu.make_async_remote_copy(
            src_ref=pieces[k], dst_ref=tall.at[:, pl.ds(first, share), :], send_sem=psend.at[k], recv_sem=precv.at[k],
            device_id={"row": row + 1 - 2 * lax.rem(row, 2)}, device_id_type=MESH,
        )

    local = [k for k in range(ranks) if pieces[k] is not None]
    crossed = [k - 1 for k in range(ranks) if pieces[k] is None]
    load_p = pltpu.make_async_copy(swap_hbm, swap, psem)
    for k in local:
        load_t(k).start()
    load_p.start()

    def load(a):
        return (
            pltpu.make_async_copy(u_hbm.at[a], ubuf.at[a], usem.at[a]),
            pltpu.make_async_copy(w_hbm.at[a], wbuf.at[a], wsem.at[a]),
        )

    def owner(k, of_side):
        return 2 * lax.rem(level + 1 + k, levels) + of_side

    for copy in load(owner(0, 1 - side)):
        copy.start()

    barrier = pltpu.get_barrier_semaphore()
    for d in range(1, n):
        pl.semaphore_signal(barrier, inc=1, device_id={"col": lax.rem(me + d, n)}, device_id_type=MESH)
    pl.semaphore_signal(barrier, inc=1, device_id={"row": row + 1 - 2 * lax.rem(row, 2)}, device_id_type=MESH)
    pl.semaphore_wait(barrier, n)

    for k in crossed:
        swap_t(k).start()
    for k in local:
        load_t(k).wait()
    load_p.wait()
    for k in range(1, levels):
        for copy in load(owner(k, 1 - side)):
            copy.start()
    for k in range(levels):
        for copy in load(owner(k, side)):
            copy.start()
    for k in crossed:
        swap_t(k).wait_recv()
    high = 256
    per = tile // high
    parts = width // wide

    def columns(c):
        return pl.ds(pl.multiple_of(c * wide, wide), wide)

    def product(a, c, out, out_at):
        at = columns(c)
        first = jnp.dot(ubuf[a], tall[:, :, at].reshape(depth, wide), preferred_element_type=F32)
        second = jnp.dot(wbuf[a], t2buf[:, at], preferred_element_type=F32)
        out[0 : 2 * half, out_at] = first[: 2 * half]
        out[2 * half : own, out_at] = first[2 * half :] + second

    def remote(source, target, sent, arrived, device):
        return pltpu.make_async_remote_copy(
            src_ref=source, dst_ref=target, send_sem=sent, recv_sem=arrived,
            device_id={"col": device}, device_id_type=MESH,
        )

    def first_copy(c, k):
        u = c * levels + k
        return (
            remote(q1s.at[u], q1r.at[u], q1a.at[u], q1b.at[u], other),
            remote(s1s.at[u], s1r.at[u], s1a.at[u], s1b.at[u], other),
        )

    def second_copy(c, k):
        device = owner(k, side)
        u = c * levels + k
        return (
            remote(q2s.at[u], q2r.at[u], q2a.at[u], q2b.at[u], device),
            remote(s2s.at[u], s2r.at[u], s2a.at[u], s2b.at[u], device),
        )

    def last_copy(c, d):
        device = lax.rem(me + d, n)
        u, v = c * n + d, c * n + n - d
        return (
            remote(xqs.at[u], xqr.at[v], xqa.at[u], xqb.at[v], device),
            remote(xss.at[u], xsr.at[v], xsa.at[u], xsb.at[v], device),
        )

    group = 128 // half
    lane, line = iota((half, 128), 1), iota((half, 128), 0)

    def to_levels(part, m):
        most = jnp.max(jnp.abs(part), axis=1, keepdims=True)
        inverse = jnp.where(most > 1e-30, LEVELS / jnp.maximum(most, 1e-30), 0.0)
        here = lane == line + (m % group) * half
        scale = jnp.sum(jnp.where(here, most * (1.0 / LEVELS), 0.0), axis=0, keepdims=True)
        return jnp.round(part * inverse).astype(I32).astype(I16), scale

    def from_levels(value, scale, m):
        here = lane == line + (m % group) * half
        return value.astype(I32).astype(F32) * jnp.sum(jnp.where(here, scale, 0.0), axis=1, keepdims=True)

    def pack(u, value, q, s):
        for g in range(0, chunks, group):
            line_of = None
            for m in range(g, min(g + group, chunks)):
                q[u, m], scale = to_levels(value(m), m)
                line_of = scale if line_of is None else line_of + scale
            s[u, g // group : g // group + 1, :] = line_of

    def unpack(u, m, q, s):
        return from_levels(q[u, m], s[u, m // group : m // group + 1, :], m)

    def rows_of(m):
        return slice(m * half, (m + 1) * half)

    @pl.loop(0, parts + 2)
    def _(turn):
        @pl.when(turn < parts)
        def _():
            at = columns(turn)

            @pl.loop(0, depth // high)
            def _(k):
                source = tall.at[k // per, pl.ds(pl.multiple_of(lax.rem(k, per) * high, high), high), :]
                t2buf[pl.ds(pl.multiple_of(k * high, high), high), at] = jnp.dot(
                    source[...], swap[:, at], preferred_element_type=F32
                ).astype(BF16)

            @pl.loop(0, levels)
            def _(k):
                @pl.when(turn == 0)
                def _():
                    for copy in load(owner(k, 1 - side)):
                        copy.wait()

                product(owner(k, 1 - side), turn, sbuf, slice(None))
                pack(turn * levels + k, lambda m: sbuf[rows_of(m), :], q1s, s1s)
                for copy in first_copy(turn, k):
                    copy.start()

        @pl.when((turn >= 1) & (turn <= parts))
        def _():
            c = turn - 1

            @pl.loop(0, levels - 1)
            def _(k):
                @pl.when(c == 0)
                def _():
                    for copy in load(owner(k, side)):
                        copy.wait()

                product(owner(k, side), c, sbuf, slice(None))
                for copy in first_copy(c, k):
                    copy.wait_recv()
                u = c * levels + k
                pack(u, lambda m: sbuf[rows_of(m), :] + unpack(u, m, q1r, s1r), q2s, s2s)
                for copy in second_copy(c, k):
                    copy.start()

        @pl.when(turn >= 2)
        def _():
            c = turn - 2

            @pl.when(c == 0)
            def _():
                for copy in load(me):
                    copy.wait()

            at = columns(c)
            product(me, c, z_ref, at)

            def take(k, q, s):
                for m in range(chunks):
                    z_ref[rows_of(m), at] += unpack(c * levels + k, m, q, s)

            for copy in first_copy(c, levels - 1):
                copy.wait_recv()
            take(levels - 1, q1r, s1r)

            @pl.loop(0, levels - 1)
            def _(k):
                for copy in second_copy(c, k):
                    copy.wait_recv()
                take(k, q2r, s2r)

            for d in range(1, n):
                xqs[c * n + d], xss[c * n + d] = to_levels(z_ref[rows_of(d + 1), at], 0)
                for copy in last_copy(c, d):
                    copy.start()

    @pl.loop(0, parts)
    def _(c):
        for d in range(1, n):
            for copy in last_copy(c, d):
                copy.wait_recv()
            v = n - d
            z_ref[own + (v - 1) * half : own + v * half, columns(c)] = from_levels(xqr[c * n + v], xsr[c * n + v], 0)

    for k in crossed:
        swap_t(k).wait_send()

    @pl.loop(0, parts)
    def _(c):
        for d in range(1, n):
            for copy in last_copy(c, d):
                copy.wait_send()

        @pl.loop(0, levels)
        def _(k):
            for copy in first_copy(c, k):
                copy.wait_send()

        @pl.loop(0, levels - 1)
        def _(k):
            for copy in second_copy(c, k):
                copy.wait_send()


def final_kernel(
    half, own, z_ref, swap_ref, place_ref, mirror_ref, pair_ref, occ_ref, out_ref, pieces, hot_own, hot_far, hot_self, pair_of
):
    rows, width = z_ref.shape

    @pl.when(pl.program_id(0) == 0)
    def _():
        rest = z_ref[...]
        for p in range(2):
            piece = rest.astype(BF16)
            pieces[p] = piece
            rest = rest - piece.astype(F32)

        same = iota((rows, rows), 0) == iota((rows, rows), 1)

        def column(row):
            return jnp.sum(jnp.where(same, row, 0.0), axis=1, keepdims=True)

        place = column(place_ref[...].astype(F32)).astype(I32)
        mirror = column(mirror_ref[...].astype(F32)).astype(I32)
        pair_of[...] = jnp.broadcast_to(column(pair_ref[...]), pair_of.shape)

        def hot(out, first):
            number = iota(out.shape, 1) + first
            out[...] = ((number == place) | (number == mirror)).astype(F32).astype(BF16)

        hot(hot_own, 0)
        hot(hot_far, own)
        hot(hot_self, rows)

    chunk = out_ref.shape[1]
    at = pl.ds(pl.multiple_of(pl.program_id(0) * chunk, chunk), chunk)
    mixer = swap_ref[...]
    total = None
    for p in (1, 0):
        far = jnp.dot(pieces[p, own:, :], mixer, preferred_element_type=F32).astype(BF16)
        near = jnp.dot(pieces[p, : 2 * half, :], mixer, preferred_element_type=F32).astype(BF16)
        term = jnp.dot(hot_own[...], pieces[p, :own, at], preferred_element_type=F32)
        mine = jnp.dot(hot_self[...], near, preferred_element_type=F32)
        other = jnp.dot(hot_far[...], far, preferred_element_type=F32)
        term = term + (mine + other)
        total = term if total is None else total + term
    out_ref[...] = total / (pair_of[:, :1] - occ_ref[...])


def body(integrals, tile_count, tile_list, amplitudes, pair_energy, occ_energy, partner):
    n = lax.axis_size("col")
    me = lax.axis_index("col")
    rows = partner.shape[0]
    half = rows // n // 2
    own = (n + 1) * half
    slots, tile = integrals.shape[2], integrals.shape[3]
    bc, _, width = amplitudes.shape
    br = slots // bc
    occ = occ_energy.shape[0]
    depth = bc * tile

    place, mirror = row_places(partner, me, n)
    ranks = lax.axis_size("row")
    pieces = [amplitudes, lax.ppermute(amplitudes, "row", [(r ^ 1, r) for r in range(ranks)])]
    for k in range(2, ranks, 2):
        pieces.append(lax.ppermute(amplitudes, "row", [((r + k) % ranks, r) for r in range(ranks)]))

    dma = pltpu.SemaphoreType.DMA
    places = pl.pallas_call(
        functools.partial(gather_kernel, n),
        out_shape=jax.ShapeDtypeStruct((n, 1, rows), I32),
        in_specs=[pl.BlockSpec(memory_space=pltpu.VMEM)],
        out_specs=pl.BlockSpec(memory_space=pltpu.VMEM),
        scratch_shapes=[pltpu.VMEM((n, 1, rows), I32), dma((n,)), dma((n,))],
        compiler_params=pltpu.CompilerParams(collective_id=1, has_side_effects=True),
        name="gather_places",
    )(place[None, :])

    number = jnp.arange(slots, dtype=I32)
    slot = jnp.sum(jnp.where(tile_list[0, 0][None, :] == number[:, None], number[None, :], 0), axis=1)

    per = tile // rows

    def tile_spec(c):
        return pl.BlockSpec((1, 1, 1, tile, tile), lambda i, s, l: (0, 0, s[i * bc + c], 0, 0))

    u, w, swap = pl.pallas_call(
        functools.partial(sort_kernel, n, half, occ, bc),
        grid_spec=pltpu.PrefetchScalarGridSpec(
            num_scalar_prefetch=2,
            grid=(br,),
            in_specs=[tile_spec(c) for c in range(bc)] + [pl.BlockSpec((n, 1, rows), lambda i, s, l: (0, 0, 0))],
            out_specs=[
                pl.BlockSpec((per, own, depth), lambda i, s, l: (i, 0, 0)),
                pl.BlockSpec((n, rows - own, depth), lambda i, s, l: (0, 0, 0)),
                pl.BlockSpec((width // br, width), lambda i, s, l: (i, 0)),
            ],
        ),
        out_shape=[
            jax.ShapeDtypeStruct((n, own, depth), BF16),
            jax.ShapeDtypeStruct((n, rows - own, depth), BF16),
            jax.ShapeDtypeStruct((width, width), BF16),
        ],
        compiler_params=pltpu.CompilerParams(vmem_limit_bytes=63 * 1024 * 1024),
        cost_estimate=pl.CostEstimate(
            flops=2 * slots * rows * tile * tile, bytes_accessed=4 * slots * tile * tile, transcendentals=0
        ),
        name="sort_rows",
    )(slot, tile_count.reshape(1), *([integrals] * bc), places)

    anywhere = pl.BlockSpec(memory_space=pl.ANY)
    wide = 256
    parts = width // wide
    scale_rows = -(-(n + 1) // (128 // half))
    units = parts * (n // 2)
    packed = [pltpu.VMEM((units, n + 1, half, wide), I16), pltpu.VMEM((units, scale_rows, 128), F32)]
    last = [pltpu.VMEM((parts * n, half, wide), I16), pltpu.VMEM((parts * n, 1, 128), F32)]
    z = pl.pallas_call(
        functools.partial(reduce_kernel, n, half, ranks, wide),
        out_shape=jax.ShapeDtypeStruct((rows, width), F32),
        in_specs=[anywhere] * (3 + len(pieces)),
        out_specs=pl.BlockSpec(memory_space=pltpu.VMEM),
        scratch_shapes=[
            pltpu.VMEM((n, own, depth), BF16),
            pltpu.VMEM((n, rows - own, depth), BF16),
            pltpu.VMEM((bc, tile, width), BF16),
            pltpu.VMEM((depth, width), BF16),
            pltpu.VMEM((width, width), BF16),
            pltpu.VMEM((own, wide), F32),
            *(packed * 4),
            *(last * 2),
            dma((n,)), dma((n,)), dma((ranks,)), dma,
            *([dma((units,))] * 8),
            *([dma((parts * n,))] * 4),
            dma((ranks,)), dma((ranks,)),
        ],
        compiler_params=pltpu.CompilerParams(
            collective_id=0, has_side_effects=True, vmem_limit_bytes=63 * 1024 * 1024
        ),
        name="reduce_pairs",
    )(u, w, swap, *pieces)

    chunk = 256
    whole = lambda k: (0, 0)
    return pl.pallas_call(
        functools.partial(final_kernel, half, own),
        grid=(width // chunk,),
        in_specs=[
            pl.BlockSpec((rows, width), whole),
            pl.BlockSpec((width, chunk), lambda k: (0, k)),
            pl.BlockSpec((1, rows), whole),
            pl.BlockSpec((1, rows), whole),
            pl.BlockSpec((1, rows), whole),
            pl.BlockSpec((1, chunk), lambda k: (0, k)),
        ],
        out_specs=pl.BlockSpec((rows, chunk), lambda k: (0, k)),
        out_shape=jax.ShapeDtypeStruct((rows, width), F32),
        scratch_shapes=[
            pltpu.VMEM((2, rows, width), BF16),
            pltpu.VMEM((rows, own), BF16),
            pltpu.VMEM((rows, rows - own), BF16),
            pltpu.VMEM((rows, 2 * half), BF16),
            pltpu.VMEM((rows, 128), F32),
        ],
        compiler_params=pltpu.CompilerParams(vmem_limit_bytes=63 * 1024 * 1024),
        name="finish_rows",
    )(
        z, swap, place[None, :], mirror[None, :], pair_energy[None, :],
        (occ_energy[:, None] + occ_energy[None, :]).reshape(1, width),
    )


def solution(mesh):
    return jax.shard_map(
        body,
        mesh=mesh,
        in_specs=(
            P("row", "col", None, None, None),
            P("row", "col"),
            P("row", "col", None),
            P("col", "row", None),
            P(("row", "col")),
            P(),
            P(("row", "col")),
        ),
        out_specs=P(("row", "col"), None),
        check_vma=False,
    )
```

profile of v0, /device:TPU:0, one launch (start us, length us, event | category | flops | bytes accessed | tf_op | source)
XLA Modules:
  0.0 132.9 jit_solution(5938570410326248127)
XLA Ops:
  0.0 0.5 collective-permute-start
  0.5 2.5 %collective-permute-start.1 = (bf16[4,128,1024]{2,1,0:T(8,128)(2,1)}, bf16[4,128,1024]{2,1,0:T(8,128)(2,1)}, u32[]{:S(2)}, u32[]{:S(2)}) collective-permute-start(bf16[4,128,1024]{2,1,0:T(8,128)(2,1)} %refs_0_.3), channel_id=1, source_target_pairs={{16,0},{24,8},{0,16},{8,24},{17,1},{25,9},{1,17},{9,25},{18,2},{26... | collective-permute-start | bytes 3145736 | tf_op jit(solution)/shard_map/ppermute | solution.py:398
  3.0 0.7 iota_select_fusion
  3.7 0.3 convert_reduce_fusion
  4.1 0.0 copy-start
  4.1 0.8 broadcast_add_fusion
  4.9 0.2 select_reduce_fusion
  5.1 1.3 select_reduce_fusion.1.slot_ref
  6.4 0.0 copy-done
  6.4 8.2 %gather_places.1.refs_4_ = s32[8,1,512]{2,1,0:T(1,128)} custom-call(s32[1,512]{1,0:T(1,128)} %bitcast.6), custom_call_target="tpu_custom_call" | custom-call | tf_op jit(solution)/shard_map/gather_places/pallas_call | solution.py:401
  15.3 0.7 add.83.occ_ref
  15.9 0.6 add_select_fusion.5
  16.5 18.1 %sort_rows.1 = (bf16[8,288,2048]{2,1,0:T(8,128)(2,1)}, bf16[8,224,2048]{2,1,0:T(8,128)(2,1)}, bf16[1024,1024]{1,0:T(8,128)(2,1)}) custom-call(s32[32]{0:T(128)} %select_reduce_fusion.1.slot_ref, s32[1]{0:T(128)} %bitcast.5.count_ref, bf16[1,1,32,512,512]{4,3,2,1,0:T(8,128)(2,1)} %refs_3_.1, bf16[1,1,32,512,512]{4,3,2,1,0:T(8,128)(2,1)} %refs_3_.1, ...), custom_call_target="tpu_custom_call" | custom-call | flops 8589934592 | bytes 33554432 | tf_op jit(solution)/shard_map/sort_rows/pallas_call | solution.py:419
  34.6 0.0 collective-permute-done.refs_1_
  34.6 0.0 collective-permute-done.1.refs_2_
  34.7 87.8 %reduce_pairs.1.z_ref = f32[512,1024]{1,0:T(8,128)} custom-call(bf16[8,288,2048]{2,1,0:T(8,128)(2,1)} %get-tuple-element.8.u_hbm, bf16[8,224,2048]{2,1,0:T(8,128)(2,1)} %get-tuple-element.9.w_hbm, bf16[1024,1024]{1,0:T(8,128)(2,1)} %get-tuple-element.10.swap_hbm.swap_ref, bf16[4,128,1024]{2,1,0:T(8,128)(2,1)} %refs_0_.3, ...), custom_call_target="tpu_custom_call" | custom-call | tf_op jit(solution)/shard_map/reduce_pairs/pallas_call | solution.py:450
  122.5 10.5 %finish_rows.1 = f32[512,1024]{1,0:T(8,128)} custom-call(f32[512,1024]{1,0:T(8,128)} %reduce_pairs.1.z_ref, bf16[1024,1024]{1,0:T(8,128)(2,1)} %get-tuple-element.10.swap_hbm.swap_ref, s32[1,512]{1,0:T(1,128)} %bitcast.7, s32[1,512]{1,0:T(1,128)} %bitcast.8, f32[1,512]{1,0:T(1,128)} %bitcast.9, f32[1,1024]{1,0:T(1,128)} %add.83.occ_ref), custom_call_target="tpu_custom_call" | custom-call | tf_op jit(solution)/shard_map/finish_rows/pallas_call | solution.py:477
  (1 shorter events, 0.0 us)
Async XLA Ops:
  0.0 34.6 %collective-permute-start = (bf16[4,128,1024]{2,1,0:T(8,128)(2,1)}, bf16[4,128,1024]{2,1,0:T(8,128)(2,1)}, u32[]{:S(2)}, u32[]{:S(2)}) collective-permute-start(bf16[4,128,1024]{2,1,0:T(8,128)(2,1)} %refs_0_.3), channel_id=1, source_target_pairs={{8,0},{0,8},{24,16},{16,24},{9,1},{1,9},{25,17},{17,25},{10,2},{2,... | collective-permute-start | bytes 3145736 | tf_op jit(solution)/shard_map/ppermute | solution.py:396
  0.5 34.2 %collective-permute-start.1 = (bf16[4,128,1024]{2,1,0:T(8,128)(2,1)}, bf16[4,128,1024]{2,1,0:T(8,128)(2,1)}, u32[]{:S(2)}, u32[]{:S(2)}) collective-permute-start(bf16[4,128,1024]{2,1,0:T(8,128)(2,1)} %refs_0_.3), channel_id=1, source_target_pairs={{16,0},{24,8},{0,16},{8,24},{17,1},{25,9},{1,17},{9,25},{18,2},{26... | collective-permute-start | bytes 3145736 | tf_op jit(solution)/shard_map/ppermute | solution.py:398
  4.1 2.4 %copy-start = (s32[512]{0:T(512)}, s32[512]{0:T(512)S(1)}, u32[]{:S(2)}) copy-start(s32[512]{0:T(512)S(1)} %select_select_fusion) | copy-start | bytes 6148
where the time goes:
time: 134 us; the launch traced here: 133 us
  Pallas kernels  125 us (93%)
  other arithmetic  3.97 us (3%)
  starting transfers between devices  3 us (2%)
    pallas_call x1, Pallas kernels, body(): pl.pallas_call(functools.partial(reduce_kernel, n, half, ranks, wide), ou...  87.8 us
    pallas_call x1, Pallas kernels, body(): pl.pallas_call(functools.partial(sort_kernel, n, half, occ, bc), grid_spe...  18.1 us
    pallas_call x1, Pallas kernels, body(): pl.pallas_call(functools.partial(final_kernel, half, own), grid=(width //...  10.5 us
    pallas_call x1, Pallas kernels, body(): pl.pallas_call(functools.partial(gather_kernel, n), out_shape=jax.ShapeDt...  8.18 us
  transfers between devices with their start and end apart: 2, of which 0 were waited for; matrix products, arithmetic and copies ran while one was open for 3% of the time, Pallas kernels for 20%

commit v1 on v0

v1 whole, which is shorter than its diff:
```python
import functools

import jax
import jax.numpy as jnp
from jax import lax
from jax.experimental import pallas as pl
from jax.experimental.pallas import tpu as pltpu
from jax.sharding import PartitionSpec as P

MESH = pl.DeviceIdType.MESH
F32, BF16, I32, I16 = jnp.float32, jnp.bfloat16, jnp.int32, jnp.int16
LEVELS = 32767.0
PIECE = 32
WIDE = 256


def iota(shape, axis):
    return lax.broadcasted_iota(I32, shape, axis)


def one_hot_of(condition):
    return condition.astype(F32).astype(BF16)


def dot(a, b):
    return jnp.dot(a, b, preferred_element_type=F32)


def dot_nt(a, b):
    return lax.dot_general(a, b, (((1,), (1,)), ((), ())), preferred_element_type=F32)


def ladder_kernel(
    n, ranks, occ, list_ref, count_ref, partner_ref, integrals, amps, out_ref,
    tiles, amp, tall, t2, u_ref, w_ref, hot_s, places, slot_s, q, mix, sbuf, z, hot, stack,
    q1s, s1s, q1r, s1r, q2s, s2s, q2r, s2r, q3s, s3s, q3r, s3r, xqs, xss, xqr, xsr,
    tile_sem, amp_sem, tsend, trecv, gsend, grecv,
    q1a, q1b, s1a, s1b, q2a, q2b, s2a, s2b, q3a, q3b, s3a, s3b, xqa, xqb, xsa, xsb,
):
    me = lax.axis_index("col")
    row = lax.axis_index("row")
    mate = row + 1 - 2 * lax.rem(row, 2)
    slots = list_ref.shape[0]
    rows = partner_ref.shape[1]
    half = rows // n // 2
    own = (n + 1) * half
    own_p = u_ref.shape[1]
    parts, bc, tile, wide = tall.shape
    depth = bc * tile
    share = amp.shape[1]
    width = amp.shape[2]
    groups = slots // 4
    m = n // 4
    hops = range(2, ranks, 2)

    def load_tiles(g):
        at = pl.ds(g * groups, groups)
        return pltpu.make_async_copy(integrals.at[0, 0, at], tiles.at[at], tile_sem.at[g])

    load_amp = pltpu.make_async_copy(amps, amp, amp_sem)
    load_amp.start()
    for g in range(4):
        load_tiles(g).start()

    barrier = pltpu.get_barrier_semaphore()
    for d in range(1, n):
        pl.semaphore_signal(barrier, inc=1, device_id={"col": lax.rem(me + d, n)}, device_id_type=MESH)
    pl.semaphore_signal(barrier, inc=1, device_id={"row": mate}, device_id_type=MESH)
    for k in hops:
        pl.semaphore_signal(barrier, inc=1, device_id={"row": lax.rem(row + k, ranks)}, device_id_type=MESH)

    def order(turn):
        return jnp.where(turn == 0, 0, jnp.where(turn == 1, parts - 1, turn - 1))

    @pl.loop(0, parts)
    def _(c):
        number = iota((width, wide), 1) + c * wide
        i = number & (occ - 1)
        s = number // occ
        q[c] = one_hot_of(iota((width, wide), 0) == i * occ + ((s - i) & (occ - 1)))
        number = iota((wide, wide), 1)
        i = number & (occ - 1)
        s = number // occ + c * (wide // occ)
        mix[c] = one_hot_of(iota((wide, wide), 0) == number - i + ((s - i) & (occ - 1)))

    def piece(c, source):
        return tall.at[c, :, pl.ds(pl.multiple_of(source * share, share), share), :]

    load_amp.wait()

    @pl.loop(0, parts)
    def _(c):
        got = dot(amp[...].reshape(bc * share, width), q[c]).astype(BF16)
        tall[c, :, pl.ds(pl.multiple_of(row * share, share), share), :] = got.reshape(bc, share, wide)

    def t_copy(c, source, slot, device):
        return pltpu.make_async_remote_copy(
            src_ref=piece(c, source), dst_ref=piece(c, source), send_sem=tsend.at[c, slot], recv_sem=trecv.at[c, source],
            device_id={"row": device}, device_id_type=MESH,
        )

    def t_direct(c):
        return [t_copy(c, row, k, lax.rem(row + k, ranks)) for k in hops] + [t_copy(c, row, 0, mate)]

    def t_forward(c):
        return [t_copy(c, lax.rem(row + ranks - k, ranks), k + 1, mate) for k in hops]

    pl.semaphore_wait(barrier, n + ranks // 2 - 1)

    @pl.loop(0, parts)
    def _(turn):
        for copy in t_direct(order(turn)):
            copy.start()

    p = partner_ref[...]
    local = lax.rem(p, n * rows)
    block = local // rows
    within = local - block * rows
    index = iota((1, rows), 1)
    key = jnp.where(block < me, within, index)
    same = iota((rows, rows), 0) == iota((rows, rows), 1)

    def column(line):
        return jnp.sum(jnp.where(same, line, 0.0), axis=1, keepdims=True)

    code = (block * rows + key).astype(F32)
    code_of = column(code)
    before = (code_of < code) & (code_of >= (block * rows).astype(F32))
    rank = jnp.sum(before.astype(F32), axis=0, keepdims=True).astype(I32)
    shift = lax.rem(block - me + n, n)
    owned = jnp.where(me < block, rank, 2 * half - 1 - rank) < half
    step = (shift - 1) * half + lax.rem(rank, half)
    place = jnp.where(block == me, rank, jnp.where(owned, 2 * half + step, own + step))
    places[me] = place

    def place_copy(d, source):
        return pltpu.make_async_remote_copy(
            src_ref=places.at[source], dst_ref=places.at[source], send_sem=gsend.at[d], recv_sem=grecv.at[source],
            device_id={"col": lax.rem(me + d, n)}, device_id_type=MESH,
        )

    for d in range(1, n):
        place_copy(d, me).start()

    tiles[slots] = jnp.zeros(tiles.shape[1:], BF16)

    @pl.loop(0, slots)
    def _(position):
        found = slots
        for s in range(slots):
            found = jnp.where((list_ref[s] == position) & (count_ref[0] > s), s, found)
        slot_s[position] = found

    for g in range(4):
        load_tiles(g).wait()
    for d in range(1, n):
        place_copy(d, lax.rem(me + d, n)).wait_recv()

    per = tile // rows

    @pl.loop(0, n)
    def _(o):
        hot_s[...] = one_hot_of(iota((rows, rows), 0) == places[o])
        part = pl.ds(pl.multiple_of(lax.rem(o, per) * rows, rows), rows)
        for c in range(bc):
            slot = slot_s[(o // per) * bc + c]
            got = dot(hot_s[...], tiles[slot, part, :]).astype(BF16)
            at = slice(c * tile, (c + 1) * tile)
            u_ref[o, :, at] = got[:own_p]
            for d in range(1, n):
                a = lax.rem(o + d, n)
                start = (n - d - 1) * half
                w_ref[a, start : start + half, at] = got[own + (d - 1) * half : own + d * half]

        @pl.when(o == n // 2)
        def _():
            for k in hops:
                t_copy(order(0), lax.rem(row + ranks - k, ranks), k, mate).wait_recv()
            for copy in t_forward(order(0)):
                copy.start()

    side = lax.rem(me, 2)
    pair = lax.rem(me // 2, 2)
    top = me // 4

    def route(c):
        swapped = jnp.where(c == parts - 1, 1, 0)
        first = side + swapped * (pair - side)
        second = pair + swapped * (side - pair)
        return first, second, 1 + swapped, 2 - swapped

    def turned(i):
        return lax.rem(top + 1 + i, m)

    def product(a, c, out):
        first = dot(u_ref[a], tall[c].reshape(depth, wide))
        out[: 2 * half, :] = first[: 2 * half]
        out[2 * half :, :] = first[2 * half :]
        out[2 * half : own, :] += dot(w_ref[a], t2[c])

    def remote(source, target, sent, arrived, device):
        return pltpu.make_async_remote_copy(
            src_ref=source, dst_ref=target, send_sem=sent, recv_sem=arrived,
            device_id={"col": device}, device_id_type=MESH,
        )

    def first_copy(c, k):
        first, _, weight, _ = route(c)
        device = me + weight * (1 - 2 * first)
        u = c * (n // 2) + k
        return (
            remote(q1s.at[u], q1r.at[u], q1a.at[u], q1b.at[u], device),
            remote(s1s.at[u], s1r.at[u], s1a.at[u], s1b.at[u], device),
        )

    def second_copy(c, i):
        _, second, _, weight = route(c)
        device = me + weight * (1 - 2 * second)
        u = c * m + i
        return (
            remote(q2s.at[u], q2r.at[u], q2a.at[u], q2b.at[u], device),
            remote(s2s.at[u], s2r.at[u], s2a.at[u], s2b.at[u], device),
        )

    def third_copy(c, i):
        device = me + 4 * (turned(i) - top)
        u = c * (m - 1) + i
        return (
            remote(q3s.at[u], q3r.at[u], q3a.at[u], q3b.at[u], device),
            remote(s3s.at[u], s3r.at[u], s3a.at[u], s3b.at[u], device),
        )

    def last_copy(c, d):
        device = lax.rem(me + d, n)
        u, v = c * n + d, c * n + n - d
        return (
            remote(xqs.at[u], xqr.at[v], xqa.at[u], xqb.at[v], device),
            remote(xss.at[u], xsr.at[v], xsa.at[u], xsb.at[v], device),
        )

    group = 128 // PIECE
    pieces = own_p // PIECE

    def here(count, k):
        return iota((count, 128), 1) == iota((count, 128), 0) + (k % group) * count

    def to_levels(part, k):
        most = jnp.max(jnp.abs(part), axis=1, keepdims=True)
        inverse = jnp.where(most > 1e-30, LEVELS / jnp.maximum(most, 1e-30), 0.0)
        scale = jnp.sum(jnp.where(here(part.shape[0], k), most * (1.0 / LEVELS), 0.0), axis=0, keepdims=True)
        return jnp.round(part * inverse).astype(I32).astype(I16), scale

    def from_levels(value, scale, k):
        return value.astype(I32).astype(F32) * jnp.sum(
            jnp.where(here(value.shape[0], k), scale, 0.0), axis=1, keepdims=True
        )

    def lines(k):
        return slice(k * PIECE, (k + 1) * PIECE)

    def pack(value, q_of, s_of):
        for g in range(0, pieces, group):
            line_of = None
            for k in range(g, min(g + group, pieces)):
                q_of[lines(k), :], scale = to_levels(value(k), k)
                line_of = scale if line_of is None else line_of + scale
            s_of[g // group : g // group + 1, :] = line_of

    def unpack(q_of, s_of, k):
        return from_levels(q_of[lines(k), :], s_of[k // group : k // group + 1, :], k)

    def start(copies):
        for copy in copies:
            copy.start()

    def arrive(copies):
        for copy in copies:
            copy.wait_recv()

    @pl.loop(0, parts)
    def _(turn):
        c = order(turn)

        @pl.when(turn < parts - 1)
        def _():
            later = order(turn + 1)
            for k in hops:
                t_copy(later, lax.rem(row + ranks - k, ranks), k, mate).wait_recv()
            for copy in t_forward(later):
                copy.start()

        t_copy(c, mate, 0, mate).wait_recv()
        for k in hops:
            t_copy(c, lax.rem(mate + ranks - k, ranks), k, mate).wait_recv()

        @pl.loop(0, bc)
        def _(k):
            at = pl.ds(pl.multiple_of(k * tile, tile), tile)
            t2[c, at, :] = dot(tall[c, k], mix[c]).astype(BF16)

        first, second, weight, other = route(c)

        @pl.loop(0, n // 2)
        def _(k):
            to = jnp.where(k < m, 1 - second, second)
            a = 4 * turned(lax.rem(k, m)) + weight * (1 - first) + other * to
            product(a, c, sbuf)
            pack(lambda j: sbuf[lines(j), :], q1s.at[c * (n // 2) + k], s1s.at[c * (n // 2) + k])
            start(first_copy(c, k))

    @pl.loop(0, parts + 4)
    def _(turn):
        @pl.when((turn >= 2) & (turn < parts + 2))
        def _():
            c = turn - 2
            first, second, weight, other = route(c)

            @pl.loop(0, m - 1)
            def _(i):
                product(4 * turned(i) + weight * first + other * second, c, sbuf)
                k = m + i
                arrive(first_copy(c, k))
                arrive(second_copy(c, i))
                u, v, x = c * (n // 2) + k, c * m + i, c * (m - 1) + i
                pack(
                    lambda j: sbuf[lines(j), :] + unpack(q1r.at[u], s1r.at[u], j) + unpack(q2r.at[v], s2r.at[v], j),
                    q3s.at[x], s3s.at[x],
                )
                start(third_copy(c, i))

        @pl.when(turn < parts)
        def _():
            c = order(turn)
            first, second, weight, other = route(c)

            @pl.loop(0, m)
            def _(i):
                product(4 * turned(i) + weight * first + other * (1 - second), c, sbuf)
                arrive(first_copy(c, i))
                u, v = c * (n // 2) + i, c * m + i
                pack(lambda j: sbuf[lines(j), :] + unpack(q1r.at[u], s1r.at[u], j), q2s.at[v], s2s.at[v])
                start(second_copy(c, i))

        @pl.when(turn == 2)
        def _():
            place_of = column(place.astype(F32))
            found = jnp.sum(
                jnp.where(iota((rows, rows), 0) == within, place_of, 0.0), axis=0, keepdims=True
            )
            mirror_of = column(jnp.where(block == me, rows + found, -1.0)).astype(I32)
            number = iota(hot.shape, 1)
            hot[...] = one_hot_of((number == place_of.astype(I32)) | (number == mirror_of))

        @pl.when((turn >= 3) & (turn < parts + 3))
        def _():
            c = turn - 3
            total = z.at[c]
            product(me, c, total)
            arrive(first_copy(c, 2 * m - 1))
            arrive(second_copy(c, m - 1))
            u, v = c * (n // 2) + 2 * m - 1, c * m + m - 1
            for i in range(m - 1):
                arrive(third_copy(c, i))
            for j in range(pieces):
                value = total[lines(j), :] + unpack(q1r.at[u], s1r.at[u], j) + unpack(q2r.at[v], s2r.at[v], j)
                for i in range(m - 1):
                    x = c * (m - 1) + i
                    value += unpack(q3r.at[x], s3r.at[x], j)
                total[lines(j), :] = value
            for d in range(1, n):
                xqs[c * n + d], xss[c * n + d] = to_levels(total[(d + 1) * half : (d + 2) * half, :], 0)
                start(last_copy(c, d))

        @pl.when(turn >= 4)
        def _():
            c = turn - 4

            def split(value, at, mixed):
                top_bits = value.astype(BF16)
                rest = (value - top_bits.astype(F32)).astype(BF16)
                for k, piece_of in ((0, top_bits), (1, rest)):
                    if mixed:
                        piece_of = dot(piece_of, mix[c]).astype(BF16)
                    stack[k, at, :] = piece_of

            split(z[c, :own, :], slice(0, own), False)
            split(z[c, : 2 * half, :], slice(rows, rows + 2 * half), True)
            for d in range(1, n):
                arrive(last_copy(c, d))
            far = jnp.concatenate([from_levels(xqr[c * n + v], xsr[c * n + v], 0) for v in range(1, n)], axis=0)
            split(far, slice(own, rows), True)
            chosen = dot(hot[...], stack[1]) + dot(hot[...], stack[0])
            top_bits = chosen.astype(BF16)
            rest = (chosen - top_bits.astype(F32)).astype(BF16)
            for k in range(0, width, wide):
                at = slice(k, k + wide)
                term = dot_nt(rest, q[c, at, :]) + dot_nt(top_bits, q[c, at, :])

                @pl.when(c == 0)
                def _():
                    out_ref[:, at] = term

                @pl.when(c > 0)
                def _():
                    out_ref[:, at] += term

    for d in range(1, n):
        place_copy(d, me).wait_send()

    @pl.loop(0, parts)
    def _(c):
        for copy in t_direct(c) + t_forward(c):
            copy.wait_send()
        for d in range(1, n):
            for copy in last_copy(c, d):
                copy.wait_send()

        @pl.loop(0, n // 2)
        def _(k):
            for copy in first_copy(c, k):
                copy.wait_send()

        @pl.loop(0, m)
        def _(i):
            for copy in second_copy(c, i):
                copy.wait_send()

        @pl.loop(0, m - 1)
        def _(i):
            for copy in third_copy(c, i):
                copy.wait_send()


def body(integrals, tile_count, tile_list, amplitudes, pair_energy, occ_energy, partner):
    n = lax.axis_size("col")
    ranks = lax.axis_size("row")
    rows = partner.shape[0]
    half = rows // n // 2
    own = (n + 1) * half
    own_p = -(-own // PIECE) * PIECE
    slots, tile = integrals.shape[2], integrals.shape[3]
    bc, share, width = amplitudes.shape
    occ = occ_energy.shape[0]
    depth = bc * tile
    parts = width // WIDE
    m = n // 4
    dma = pltpu.SemaphoreType.DMA
    lines = -(-own_p // 128)

    def packed(units):
        return [pltpu.VMEM((units, own_p, WIDE), I16), pltpu.VMEM((units, lines, 128), F32)] * 2

    def sems(units):
        return [dma((units,))] * 4

    counts = (parts * n // 2, parts * m, parts * (m - 1))
    anywhere = pl.BlockSpec(memory_space=pl.ANY)
    scalars = pl.BlockSpec(memory_space=pltpu.SMEM)
    vector = pl.BlockSpec(memory_space=pltpu.VMEM)
    total = pl.pallas_call(
        functools.partial(ladder_kernel, n, ranks, occ),
        out_shape=jax.ShapeDtypeStruct((rows, width), F32),
        in_specs=[scalars, scalars, vector, anywhere, anywhere],
        out_specs=vector,
        scratch_shapes=[
            pltpu.VMEM((slots + 1, tile, tile), BF16),
            pltpu.VMEM((bc, share, width), BF16),
            pltpu.VMEM((parts, bc, tile, WIDE), BF16),
            pltpu.VMEM((parts, depth, WIDE), BF16),
            pltpu.VMEM((n, own_p, depth), BF16),
            pltpu.VMEM((n, rows - own, depth), BF16),
            pltpu.VMEM((rows, rows), BF16),
            pltpu.VMEM((n, 1, rows), I32),
            pltpu.SMEM((slots,), I32),
            pltpu.VMEM((parts, width, WIDE), BF16),
            pltpu.VMEM((parts, WIDE, WIDE), BF16),
            pltpu.VMEM((own_p, WIDE), F32),
            pltpu.VMEM((parts, own_p, WIDE), F32),
            pltpu.VMEM((rows, rows + 2 * half), BF16),
            pltpu.VMEM((2, rows + 2 * half, WIDE), BF16),
            *packed(counts[0]), *packed(counts[1]), *packed(counts[2]),
            *([pltpu.VMEM((parts * n, half, WIDE), I16), pltpu.VMEM((parts * n, 1, 128), F32)] * 2),
            dma((4,)), dma, dma((parts, ranks)), dma((parts, ranks)), dma((n,)), dma((n,)),
            *sems(counts[0]), *sems(counts[1]), *sems(counts[2]), *sems(parts * n),
        ],
        compiler_params=pltpu.CompilerParams(
            collective_id=0, has_side_effects=True, vmem_limit_bytes=63 * 1024 * 1024
        ),
        name="ladder",
    )(tile_list.reshape(slots), tile_count.reshape(1), partner[None, :], integrals, amplitudes)
    pairs = (occ_energy[:, None] + occ_energy[None, :]).reshape(1, width)
    return total / (pair_energy[:, None] - pairs)


def solution(mesh):
    return jax.shard_map(
        body,
        mesh=mesh,
        in_specs=(
            P("row", "col", None, None, None),
            P("row", "col"),
            P("row", "col", None),
            P("col", "row", None),
            P(("row", "col")),
            P(),
            P(("row", "col")),
        ),
        out_specs=P(("row", "col"), None),
        check_vma=False,
    )
```

time: 134 us -> 107 us (0.80)
  Pallas kernels: 125 us -> 102 us
  starting transfers between devices: 3 us -> 0 us
    pallas_call x4 -> x1, Pallas kernels: 125 us -> 102 us  [body(): pl.pallas_call(functools.partial(ladder_kernel, n, ranks, occ), out_shape...]
    div x0 -> x1, other arithmetic: none -> 3.26 us  [body(): return total / (pair_energy[:, None] - pairs)]
    ppermute x2 -> x0, starting transfers between devices: 3 us -> none  [the longest x1 2.51 us: body(): lax.ppermute(amplitudes, 'row', [((r + k) % ranks, r) for r in range(rank...]
    reduce_sum x3 -> x0, other arithmetic: 1.88 us -> none  [the longest x1 1.29 us: body(): jnp.sum(jnp.where(tile_list[0, 0][None, :] == number[:, None], number[Non...]
  transfers between devices with their start and end apart: 2 -> 0, of which waited for: 0 -> 0; matrix products, arithmetic and copies ran while one was open for 3% -> 0% of each run, Pallas kernels for 20% -> 0%
where the time goes in v1:
time: 107 us
  Pallas kernels  102 us (95%)
  other arithmetic  4.06 us (4%)
    pallas_call x1, Pallas kernels, body(): pl.pallas_call(functools.partial(ladder_kernel, n, ranks, occ), out_shape...  102 us
    div x1, other arithmetic, body(): return total / (pair_energy[:, None] - pairs)  3.26 us

profile of v1, /device:TPU:0, one launch (start us, length us, event | category | flops | bytes accessed | tf_op | source)
XLA Modules:
  0.0 106.9 jit_solution(3884677636020485740)
XLA Ops:
  0.7 0.8 broadcast_add_fusion
  1.5 0.1 add.23
  1.5 0.0 copy-start
  1.5 102.1 %ladder.1 = f32[512,1024]{1,0:T(8,128)} custom-call(s32[32]{0:T(128)} %bitcast.5, s32[1]{0:T(128)} %bitcast.3.count_ref, s32[1,512]{1,0:T(1,128)} %bitcast.4, bf16[1,1,32,512,512]{4,3,2,1,0:T(8,128)(2,1)} %integrals.1, bf16[4,128,1024]{2,1,0:T(8,128)(2,1)} %amps.1), custom_call_target="tpu_custom_call" | custom-call | tf_op jit(solution)/shard_map/ladder/pallas_call | solution.py:460
  103.6 0.0 copy-done
  103.6 3.3 %subtract_divide_fusion = f32[512,1024]{1,0:T(8,128)} fusion(f32[512,1024]{1,0:T(8,128)} %ladder.1, f32[1024]{0:T(1024)S(1)} %add.23, f32[512]{0:T(512)S(1)} %copy-done), kind=kLoop, calls=%fused_computation | loop fusion | flops 1048576 | bytes 4200448 | tf_op jit(solution)/shard_map/div | solution.py:492
Async XLA Ops:
  1.5 102.1 %copy-start = (f32[512]{0:T(512)S(1)}, f32[512]{0:T(512)}, u32[]{:S(2)}) copy-start(f32[512]{0:T(512)} %param.11) | copy-start | bytes 6148

commit v2 on v1

v2 whole, which is shorter than its diff:
```python
import functools

import jax
import jax.numpy as jnp
from jax import lax
from jax.experimental import pallas as pl
from jax.experimental.pallas import tpu as pltpu
from jax.sharding import PartitionSpec as P

MESH = pl.DeviceIdType.MESH
F32, BF16, I32, I16 = jnp.float32, jnp.bfloat16, jnp.int32, jnp.int16
LEVELS = 32767.0
PIECE = 32
WIDE = 256


def schedule(parts, n):
    m = n // 4
    counts = {1: n // 2, 2: m, 3: m - 1}
    first, rest = slice(0, 1), slice(1, None)
    blocks = [(1, 0), (1, 1), (2, 1), (1, 2, first), (2, 0), (1, 2, rest), (3, 1), (1, 3), (3, 0), (2, 2), (0, 0), (4, 1), (3, 2)]
    blocks += [(2, 3), (4, 0), (5, 1), (3, 3), (4, 2), (5, 0), (4, 3), (5, 2), (5, 3)]
    if parts != 4:
        blocks = [(0, 0)] + [(kind, c) for kind in range(1, 6) for c in range(parts)]
    return [(kind, c, k) for kind, c, *some in blocks for k in list(range(counts.get(kind, 1)))[some[0] if some else slice(None)]]


def iota(shape, axis):
    return lax.broadcasted_iota(I32, shape, axis)


def one_hot_of(condition):
    return condition.astype(F32).astype(BF16)


def dot(a, b):
    return jnp.dot(a, b, preferred_element_type=F32)


def dot_nt(a, b):
    return lax.dot_general(a, b, (((1,), (1,)), ((), ())), preferred_element_type=F32)


def ladder_kernel(
    n, ranks, occ, list_ref, count_ref, partner_ref, integrals, amps, out_ref,
    tiles, amp, tall, t2, u_ref, w_ref, hot_u, hot_w, places, slot_s, q, mix, sbuf, z, hot_near, hot_far, near, chosen,
    qs, ss, qr, sr, xqs, xss, xqr, xsr,
    tile_sem, amp_sem, tsend, trecv, gsend, grecv, q_sent, s_sent, q_here, s_here, xq_sent, xs_sent, xq_here, xs_here,
):
    me = lax.axis_index("col")
    row = lax.axis_index("row")
    mate = row + 1 - 2 * lax.rem(row, 2)
    slots = list_ref.shape[0]
    rows = partner_ref.shape[1]
    half = rows // n // 2
    own = (n + 1) * half
    own_p = u_ref.shape[1]
    parts, bc, tile, wide = tall.shape
    depth = bc * tile
    share = amp.shape[1]
    width = amp.shape[2]
    groups = slots // 4
    m = n // 4
    hops = range(2, ranks, 2)

    def load_tiles(g):
        at = pl.ds(g * groups, groups)
        return pltpu.make_async_copy(integrals.at[0, 0, at], tiles.at[at], tile_sem.at[g])

    load_amp = pltpu.make_async_copy(amps, amp, amp_sem)
    load_amp.start()
    for g in range(4):
        load_tiles(g).start()

    barrier = pltpu.get_barrier_semaphore()
    for d in range(1, n):
        pl.semaphore_signal(barrier, inc=1, device_id={"col": lax.rem(me + d, n)}, device_id_type=MESH)
    pl.semaphore_signal(barrier, inc=1, device_id={"row": mate}, device_id_type=MESH)
    for k in hops:
        pl.semaphore_signal(barrier, inc=1, device_id={"row": lax.rem(row + k, ranks)}, device_id_type=MESH)

    def piece(c, source):
        return tall.at[c, :, pl.ds(pl.multiple_of(source * share, share), share), :]

    def t_copy(c, source, device):
        return pltpu.make_async_remote_copy(
            src_ref=piece(c, source), dst_ref=piece(c, source), send_sem=tsend, recv_sem=trecv.at[c, source],
            device_id={"row": device}, device_id_type=MESH,
        )

    def t_direct(c):
        return [t_copy(c, row, lax.rem(row + k, ranks)) for k in hops] + [t_copy(c, row, mate)]

    def t_forward(c):
        return [t_copy(c, lax.rem(row + ranks - k, ranks), mate) for k in hops]

    def reorder(c):
        number = iota((width, wide), 1) + c * wide
        i = number & (occ - 1)
        s = number // occ
        q[...] = one_hot_of(iota((width, wide), 0) == i * occ + ((s - i) & (occ - 1)))
        got = dot(amp[...].reshape(bc * share, width), q[...]).astype(BF16)
        tall[c, :, pl.ds(pl.multiple_of(row * share, share), share), :] = got.reshape(bc, share, wide)

    load_amp.wait()

    @pl.loop(0, parts)
    def _(turn):
        reorder(turn)

        @pl.when(turn == 0)
        def _():
            pl.semaphore_wait(barrier, n + ranks // 2 - 1)

        for copy in t_direct(turn):
            copy.start()

    p = partner_ref[...]
    local = lax.rem(p, n * rows)
    block = local // rows
    within = local - block * rows
    index = iota((1, rows), 1)
    key = jnp.where(block < me, within, index)
    same = iota((rows, rows), 0) == iota((rows, rows), 1)

    def column(line):
        return jnp.sum(jnp.where(same, line, 0.0), axis=1, keepdims=True)

    code = (block * rows + key).astype(F32)
    code_of = column(code)
    before = (code_of < code) & (code_of >= (block * rows).astype(F32))
    rank = jnp.sum(before.astype(F32), axis=0, keepdims=True).astype(I32)
    shift = lax.rem(block - me + n, n)
    owned = jnp.where(me < block, rank, 2 * half - 1 - rank) < half
    step = (shift - 1) * half + lax.rem(rank, half)
    place = jnp.where(block == me, rank, jnp.where(owned, 2 * half + step, own + step))
    places[me] = place

    def place_copy(d, source):
        return pltpu.make_async_remote_copy(
            src_ref=places.at[source], dst_ref=places.at[source], send_sem=gsend, recv_sem=grecv.at[source],
            device_id={"col": lax.rem(me + d, n)}, device_id_type=MESH,
        )

    for d in range(1, n):
        place_copy(d, me).start()

    tiles[slots] = jnp.zeros(tiles.shape[1:], BF16)

    @pl.loop(0, parts)
    def _(c):
        number = iota((wide, wide), 1)
        i = number & (occ - 1)
        s = number // occ + c * (wide // occ)
        mix[c] = one_hot_of(iota((wide, wide), 0) == number - i + ((s - i) & (occ - 1)))

    @pl.loop(0, slots)
    def _(position):
        found = slots
        for s in range(slots):
            found = jnp.where((list_ref[s] == position) & (count_ref[0] > s), s, found)
        slot_s[position] = found

    for g in range(4):
        load_tiles(g).wait()
    for d in range(1, n):
        place_copy(d, lax.rem(me + d, n)).wait_recv()

    per = tile // rows

    def sort(o, hot, first, store):
        hot[...] = one_hot_of(iota(hot.shape, 0) + first == places[o])
        part = pl.ds(pl.multiple_of(lax.rem(o, per) * rows, rows), rows)

        for c in range(bc):
            slot = slot_s[(o // per) * bc + c]
            store(dot(hot[...], tiles[slot, part, :]).astype(BF16), slice(c * tile, (c + 1) * tile))

    def sort_u(o):
        def store(got, at):
            u_ref[o, :, at] = got

        sort(o, hot_u, 0, store)

    @pl.loop(0, n)
    def _(o):
        def store(got, at):
            for d in range(1, n):
                a = lax.rem(o + d, n)
                start = (n - d - 1) * half
                w_ref[a, start : start + half, at] = got[(d - 1) * half : d * half]

        sort(o, hot_w, own, store)

        @pl.when(o == n // 2)
        def _():
            for k in hops:
                t_copy(0, lax.rem(row + ranks - k, ranks), mate).wait_recv()
            for copy in t_forward(0):
                copy.start()

    side = lax.rem(me, 2)
    pair = lax.rem(me // 2, 2)
    top = me // 4

    def route(c):
        swapped = jnp.where(c == 1, 1, 0)
        first = side + swapped * (pair - side)
        second = pair + swapped * (side - pair)
        return first, second, 1 + swapped, 2 - swapped

    def turned(i):
        return lax.rem(top + 1 + i, m)

    def product(a, c, out):
        first = dot(u_ref[a], tall[c].reshape(depth, wide))
        out[: 2 * half, :] = first[: 2 * half]
        out[2 * half :, :] = first[2 * half :]
        out[2 * half : own, :] += dot(w_ref[a], t2[c])

    def remote(source, target, sent, arrived, device):
        return pltpu.make_async_remote_copy(
            src_ref=source, dst_ref=target, send_sem=sent, recv_sem=arrived,
            device_id={"col": device}, device_id_type=MESH,
        )

    def unit_copies(u, device):
        return (
            remote(qs.at[u], qr.at[u], q_sent, q_here.at[u], device),
            remote(ss.at[u], sr.at[u], s_sent, s_here.at[u], device),
        )

    def last_copy(c, d):
        device = lax.rem(me + d, n)
        u, v = c * (n - 1) + d - 1, c * (n - 1) + n - d - 1
        return (
            remote(xqs.at[u], xqr.at[v], xq_sent, xq_here.at[c], device),
            remote(xss.at[u], xsr.at[v], xs_sent, xs_here.at[c], device),
        )

    def last_arrive(c):
        at = pl.ds(c * (n - 1), n - 1)
        device = lax.rem(me + 1, n)
        remote(xqs.at[at], xqr.at[at], xq_sent, xq_here.at[c], device).wait_recv()
        remote(xss.at[at], xsr.at[at], xs_sent, xs_here.at[c], device).wait_recv()

    group = 128 // PIECE
    pieces = own_p // PIECE

    def here(count, k):
        return iota((count, 128), 1) == iota((count, 128), 0) + (k % group) * count

    def to_levels(part, k):
        most = jnp.max(jnp.abs(part), axis=1, keepdims=True)
        inverse = jnp.where(most > 1e-30, LEVELS / jnp.maximum(most, 1e-30), 0.0)
        scale = jnp.sum(jnp.where(here(part.shape[0], k), most * (1.0 / LEVELS), 0.0), axis=0, keepdims=True)
        return jnp.round(part * inverse).astype(I32).astype(I16), scale

    def from_levels(value, scale, k):
        return value.astype(I32).astype(F32) * jnp.sum(
            jnp.where(here(value.shape[0], k), scale, 0.0), axis=1, keepdims=True
        )

    def lines(k):
        return slice(k * PIECE, (k + 1) * PIECE)

    def pack(u):
        for g in range(0, pieces, group):
            line_of = None
            for k in range(g, min(g + group, pieces)):
                qs[u, lines(k), :], scale = to_levels(sbuf[lines(k), :], k)
                line_of = scale if line_of is None else line_of + scale
            ss[u, g // group : g // group + 1, :] = line_of

    def add(u):
        for k in range(pieces):
            sbuf[lines(k), :] += from_levels(qr[u, lines(k), :], sr[u, k // group : k // group + 1, :], k)

    def start(copies):
        for copy in copies:
            copy.start()

    def arrive(copies):
        for copy in copies:
            copy.wait_recv()

    def amplitudes_of(c):
        @pl.when(c < parts - 1)
        def _():
            later = c + 1
            for k in hops:
                t_copy(later, lax.rem(row + ranks - k, ranks), mate).wait_recv()
            for copy in t_forward(later):
                copy.start()

        t_copy(c, mate, mate).wait_recv()
        for k in hops:
            t_copy(c, lax.rem(mate + ranks - k, ranks), mate).wait_recv()

        @pl.loop(0, bc)
        def _(k):
            at = pl.ds(pl.multiple_of(k * tile, tile), tile)
            t2[c, at, :] = dot(tall[c, k], mix[c]).astype(BF16)

    def unit(kind, c, k):
        def pick(*values):
            got = values[0]
            for at, value in enumerate(values[1:]):
                got = jnp.where(kind == at + 2, value, got)
            return got

        first, second, weight, other = route(c)
        on_first = pick(1 - first, first, first, first)
        on_second = pick(jnp.where(k < m, 1 - second, second), 1 - second, second, second)
        beside = jnp.where(kind == 4, m - 1, lax.rem(k, m))
        level = turned(beside)
        a = 4 * level + weight * on_first + other * on_second

        @pl.when((kind == 1) & (k == 0))
        def _():
            amplitudes_of(c)

        @pl.when((kind == 1) & ((c == 0) | ((c == 1) & (k >= m))))
        def _():
            sort_u(a)

        product(a, c, sbuf)
        base = c * (n - 1)

        @pl.loop(0, jnp.where(kind == 4, m + 1, kind - 1))
        def _(at):
            u = jnp.where(
                at == 0, pick(0, k, m + k, 2 * m - 1), jnp.where(at == 1, 2 * m + beside, 3 * m + at - 2)
            )
            arrive(unit_copies(base + u, me + 1 - 2 * side))
            add(base + u)

        @pl.when(kind < 4)
        def _():
            u = base + pick(k, 2 * m + k, 3 * m + k)
            pack(u)
            start(unit_copies(u, me + pick(weight * (1 - 2 * first), other * (1 - 2 * second), 4 * (level - top))))

        @pl.when((kind == 1) & (c == 1) & (k >= m))
        def _():
            sort_u(4 * level + side + 2 * pair)

        @pl.when(kind == 4)
        def _():
            z[c] = sbuf[...]
            for d in range(1, n):
                u = c * (n - 1) + d - 1
                xqs[u], xss[u] = to_levels(sbuf[(d + 1) * half : (d + 2) * half, :], 0)
                start(last_copy(c, d))

    def prepare():
        place_of = column(place.astype(F32))
        found = jnp.sum(jnp.where(iota((rows, rows), 0) == within, place_of, 0.0), axis=0, keepdims=True)
        mirror_of = column(jnp.where(block == me, rows + found, -1.0)).astype(I32)
        place_of = place_of.astype(I32)
        number = iota(hot_near.shape, 1)
        number = jnp.where(number < own, number, number + rows - own)
        hot_near[...] = one_hot_of((number == place_of) | (number == mirror_of))
        hot_far[...] = one_hot_of(iota(hot_far.shape, 1) + own == place_of)

    def halves(value):
        high = value.astype(BF16)
        return high, (value - high.astype(F32)).astype(BF16)

    def assemble(c):
        for k, half_of in enumerate(halves(z[c, :own, :])):
            near[k, :own, :] = half_of
        for k, half_of in enumerate(halves(z[c, : 2 * half, :])):
            near[k, own:, :] = dot(half_of, mix[c]).astype(BF16)
        chosen[...] = dot(hot_near[...], near[1]) + dot(hot_near[...], near[0])
        last_arrive(c)
        at = c * (n - 1)
        far = jnp.concatenate([from_levels(xqr[at + v], xsr[at + v], 0) for v in range(n - 1)], axis=0)
        high, low = [dot(half_of, mix[c]).astype(BF16) for half_of in halves(far)]
        out_ref[:, pl.ds(pl.multiple_of(c * wide, wide), wide)] = chosen[...] + (dot(hot_far[...], low) + dot(hot_far[...], high))

    table = [(kind * parts + turn) * n + k for kind, turn, k in schedule(parts, n)]

    @pl.loop(0, len(table))
    def _(step):
        entry = 0
        for at, value in enumerate(table):
            entry = jnp.where(step == at, value, entry)
        k = lax.rem(entry, n)
        turn = lax.rem(entry // n, parts)
        kind = entry // (n * parts)
        pl.when(kind == 0)(prepare)
        pl.when((kind > 0) & (kind < 5))(lambda: unit(kind, turn, k))
        pl.when(kind == 5)(lambda: assemble(turn))

    def sent(source, semaphore):
        pltpu.make_async_remote_copy(
            src_ref=source, dst_ref=source, send_sem=semaphore, recv_sem=amp_sem,
            device_id={"row": mate}, device_id_type=MESH,
        ).wait_send()

    sent(places.at[: n - 1], gsend)
    sent(tall.at[:, :, : share * (ranks - 1), :], tsend)
    for source, semaphore in ((qs, q_sent), (ss, s_sent), (xqs, xq_sent), (xss, xs_sent)):
        sent(source, semaphore)


def finish_kernel(occ, occ_ref, pair_ref, chosen_ref, out_ref, pieces, pair_of):
    rows, width = chosen_ref.shape
    wide = out_ref.shape[1]

    @pl.when(pl.program_id(0) == 0)
    def _():
        value = chosen_ref[...]
        high = value.astype(BF16)
        pieces[0] = high
        pieces[1] = (value - high.astype(F32)).astype(BF16)
        same = iota((rows, rows), 0) == iota((rows, rows), 1)
        pair_of[...] = jnp.broadcast_to(jnp.sum(jnp.where(same, pair_ref[...], 0.0), axis=1, keepdims=True), pair_of.shape)

    number = iota((1, wide), 1) + pl.program_id(0) * wide
    i, j = number // occ, number & (occ - 1)
    turned = one_hot_of(iota((width, wide), 0) == ((i + j) & (occ - 1)) * occ + i)
    first, second = jnp.zeros((1, wide), F32), jnp.zeros((1, wide), F32)
    for k in range(occ):
        first += jnp.where(i == k, occ_ref[k], 0.0)
        second += jnp.where(j == k, occ_ref[k], 0.0)
    total = dot(pieces[1], turned) + dot(pieces[0], turned)
    out_ref[...] = total / (pair_of[:, :1] - (first + second))


def body(integrals, tile_count, tile_list, amplitudes, pair_energy, occ_energy, partner):
    n = lax.axis_size("col")
    ranks = lax.axis_size("row")
    rows = partner.shape[0]
    half = rows // n // 2
    own = (n + 1) * half
    own_p = -(-own // PIECE) * PIECE
    slots, tile = integrals.shape[2], integrals.shape[3]
    bc, share, width = amplitudes.shape
    depth = bc * tile
    parts = width // WIDE
    occ = occ_energy.shape[0]
    dma = pltpu.SemaphoreType.DMA
    lines = -(-own_p // 128)

    units = parts * (n - 1)
    anywhere = pl.BlockSpec(memory_space=pl.ANY)
    scalars = pl.BlockSpec(memory_space=pltpu.SMEM)
    vector = pl.BlockSpec(memory_space=pltpu.VMEM)
    chosen = pl.pallas_call(
        functools.partial(ladder_kernel, n, ranks, occ),
        out_shape=jax.ShapeDtypeStruct((rows, width), F32),
        in_specs=[scalars, scalars, vector, anywhere, anywhere],
        out_specs=vector,
        scratch_shapes=[
            pltpu.VMEM((slots + 1, tile, tile), BF16),
            pltpu.VMEM((bc, share, width), BF16),
            pltpu.VMEM((parts, bc, tile, WIDE), BF16),
            pltpu.VMEM((parts, depth, WIDE), BF16),
            pltpu.VMEM((n, own_p, depth), BF16),
            pltpu.VMEM((n, rows - own, depth), BF16),
            pltpu.VMEM((own_p, rows), BF16),
            pltpu.VMEM((rows - own, rows), BF16),
            pltpu.VMEM((n, 1, rows), I32),
            pltpu.SMEM((slots,), I32),
            pltpu.VMEM((width, WIDE), BF16),
            pltpu.VMEM((parts, WIDE, WIDE), BF16),
            pltpu.VMEM((own_p, WIDE), F32),
            pltpu.VMEM((parts, own_p, WIDE), F32),
            pltpu.VMEM((rows, own + 2 * half), BF16),
            pltpu.VMEM((rows, rows - own), BF16),
            pltpu.VMEM((2, own + 2 * half, WIDE), BF16),
            pltpu.VMEM((rows, WIDE), F32),
            *([pltpu.VMEM((units, own_p, WIDE), I16), pltpu.VMEM((units, -(-own_p // 128), 128), F32)] * 2),
            *([pltpu.VMEM((units, half, WIDE), I16), pltpu.VMEM((units, 1, 128), F32)] * 2),
            dma((4,)), dma, dma, dma((parts, ranks)), dma, dma((n,)),
            dma, dma, dma((units,)), dma((units,)), dma, dma, dma((parts,)), dma((parts,)),
        ],
        compiler_params=pltpu.CompilerParams(
            collective_id=0, has_side_effects=True, vmem_limit_bytes=63 * 1024 * 1024
        ),
        name="ladder",
    )(tile_list.reshape(slots), tile_count.reshape(1), partner[None, :], integrals, amplitudes)

    whole = lambda k: (0, 0)
    return pl.pallas_call(
        functools.partial(finish_kernel, occ),
        grid=(parts,),
        in_specs=[scalars, pl.BlockSpec((1, rows), whole), pl.BlockSpec((rows, width), whole)],
        out_specs=pl.BlockSpec((rows, WIDE), lambda k: (0, k)),
        out_shape=jax.ShapeDtypeStruct((rows, width), F32),
        scratch_shapes=[pltpu.VMEM((2, rows, width), BF16), pltpu.VMEM((rows, 128), F32)],
        name="finish",
    )(occ_energy, pair_energy[None, :], chosen)


def solution(mesh):
    return jax.shard_map(
        body,
        mesh=mesh,
        in_specs=(
            P("row", "col", None, None, None),
            P("row", "col"),
            P("row", "col", None),
            P("col", "row", None),
            P(("row", "col")),
            P(),
            P(("row", "col")),
        ),
        out_specs=P(("row", "col"), None),
        check_vma=False,
    )
```

time: 107 us -> 102 us (0.953)
  other arithmetic: 4.06 us -> 0 us
    pallas_call x1, Pallas kernels: 102 us -> 95.2 us  [body(): pl.pallas_call(functools.partial(ladder_kernel, n, ranks, occ), out_shape...]
    pallas_call x0 -> x1, Pallas kernels: none -> 6.04 us  [body(): pl.pallas_call(functools.partial(finish_kernel, occ), grid=(parts,), in_s...]
    div x1 -> x0, other arithmetic: 3.26 us -> none  [body(): return total / (pair_energy[:, None] - pairs)]
where the time goes in v2:
time: 102 us
  Pallas kernels  101 us (99%)
    pallas_call x1, Pallas kernels, body(): pl.pallas_call(functools.partial(ladder_kernel, n, ranks, occ), out_shape...  95.2 us
    pallas_call x1, Pallas kernels, body(): pl.pallas_call(functools.partial(finish_kernel, occ), grid=(parts,), in_s...  6.04 us

profile of v2, /device:TPU:0, one launch (start us, length us, event | category | flops | bytes accessed | tf_op | source)
XLA Modules:
  0.0 101.9 jit_solution(2707651789679840061)
XLA Ops:
  0.7 95.2 %ladder.1.chosen_ref = f32[512,1024]{1,0:T(8,128)} custom-call(s32[32]{0:T(128)} %bitcast.7, s32[1]{0:T(128)} %bitcast.4.count_ref, s32[1,512]{1,0:T(1,128)} %bitcast.6, bf16[1,1,32,512,512]{4,3,2,1,0:T(8,128)(2,1)} %integrals.1, bf16[4,128,1024]{2,1,0:T(8,128)(2,1)} %amps.1), custom_call_target="tpu_custom_call" | custom-call | tf_op jit(solution)/shard_map/ladder/pallas_call | solution.py:451
  95.9 6.0 %finish.1 = f32[512,1024]{1,0:T(8,128)} custom-call(f32[32]{0:T(128)} %occ_ref.1, f32[1,512]{1,0:T(1,128)} %bitcast.5, f32[512,1024]{1,0:T(8,128)} %ladder.1.chosen_ref), custom_call_target="tpu_custom_call" | custom-call | tf_op jit(solution)/shard_map/finish/pallas_call | solution.py:487

commit v3 on v2

--- a/solution.py
+++ b/solution.py
@@ -19,7 +19,7 @@
     counts = {1: n // 2, 2: m, 3: m - 1}
     first, rest = slice(0, 1), slice(1, None)
     blocks = [(1, 0), (1, 1), (2, 1), (1, 2, first), (2, 0), (1, 2, rest), (3, 1), (1, 3), (3, 0), (2, 2), (0, 0), (4, 1), (3, 2)]
-    blocks += [(2, 3), (4, 0), (5, 1), (3, 3), (4, 2), (5, 0), (4, 3), (5, 2), (5, 3)]
+    blocks += [(4, 0), (2, 3), (5, 1), (3, 3), (4, 2), (5, 0), (4, 3), (5, 2), (5, 3)]
     if parts != 4:
         blocks = [(0, 0)] + [(kind, c) for kind in range(1, 6) for c in range(parts)]
     return [(kind, c, k) for kind, c, *some in blocks for k in list(range(counts.get(kind, 1)))[some[0] if some else slice(None)]]
@@ -37,13 +37,15 @@
     return jnp.dot(a, b, preferred_element_type=F32)
 
 
-def dot_nt(a, b):
-    return lax.dot_general(a, b, (((1,), (1,)), ((), ())), preferred_element_type=F32)
+def unsort(c, wide, width, occ):
+    number = iota((1, width), 1)
+    i, j = number // occ, number & (occ - 1)
+    return one_hot_of(iota((wide, width), 0) + c * wide == ((i + j) & (occ - 1)) * occ + i)
 
 
 def ladder_kernel(
-    n, ranks, occ, list_ref, count_ref, partner_ref, integrals, amps, out_ref,
-    tiles, amp, tall, t2, u_ref, w_ref, hot_u, hot_w, places, slot_s, q, mix, sbuf, z, hot_near, hot_far, near, chosen,
+    n, ranks, occ, list_ref, count_ref, partner_ref, integrals, amps, out_ref, last_ref,
+    tiles, amp, tall, t2, u_ref, w_ref, hot_u, hot_w, places, slot_s, q, mix, sbuf, z, hot_near, hot_far, near, chosen, turned_q,
     qs, ss, qr, sr, xqs, xss, xqr, xsr,
     tile_sem, amp_sem, tsend, trecv, gsend, grecv, q_sent, s_sent, q_here, s_here, xq_sent, xs_sent, xq_here, xs_here,
 ):
@@ -362,6 +364,11 @@
         number = jnp.where(number < own, number, number + rows - own)
         hot_near[...] = one_hot_of((number == place_of) | (number == mirror_of))
         hot_far[...] = one_hot_of(iota(hot_far.shape, 1) + own == place_of)
+        out_ref[...] = jnp.zeros(out_ref.shape, F32)
+
+        @pl.loop(0, parts - 1)
+        def _(c):
+            turned_q[c] = unsort(c, wide, width, occ)
 
     def halves(value):
         high = value.astype(BF16)
@@ -377,7 +384,18 @@
         at = c * (n - 1)
         far = jnp.concatenate([from_levels(xqr[at + v], xsr[at + v], 0) for v in range(n - 1)], axis=0)
         high, low = [dot(half_of, mix[c]).astype(BF16) for half_of in halves(far)]
-        out_ref[:, pl.ds(pl.multiple_of(c * wide, wide), wide)] = chosen[...] + (dot(hot_far[...], low) + dot(hot_far[...], high))
+        chosen[...] += dot(hot_far[...], low) + dot(hot_far[...], high)
+
+        @pl.when(c == parts - 1)
+        def _():
+            last_ref[...] = chosen[...]
+
+        @pl.when(c < parts - 1)
+        def _():
+            high, low = halves(chosen[...])
+            for k in range(0, width, wide):
+                at = slice(k, k + wide)
+                out_ref[:, at] += dot(low, turned_q[c, :, at]) + dot(high, turned_q[c, :, at])
 
     table = [(kind * parts + turn) * n + k for kind, turn, k in schedule(parts, n)]
 
@@ -405,28 +423,28 @@
         sent(source, semaphore)
 
 
-def finish_kernel(occ, occ_ref, pair_ref, chosen_ref, out_ref, pieces, pair_of):
-    rows, width = chosen_ref.shape
-    wide = out_ref.shape[1]
+def finish_kernel(occ, occ_ref, pair_ref, sum_ref, last_ref, out_ref, turned_q, energy):
+    lines, width = sum_ref.shape
+    wide = last_ref.shape[1]
 
     @pl.when(pl.program_id(0) == 0)
     def _():
-        value = chosen_ref[...]
-        high = value.astype(BF16)
-        pieces[0] = high
-        pieces[1] = (value - high.astype(F32)).astype(BF16)
-        same = iota((rows, rows), 0) == iota((rows, rows), 1)
-        pair_of[...] = jnp.broadcast_to(jnp.sum(jnp.where(same, pair_ref[...], 0.0), axis=1, keepdims=True), pair_of.shape)
-
-    number = iota((1, wide), 1) + pl.program_id(0) * wide
-    i, j = number // occ, number & (occ - 1)
-    turned = one_hot_of(iota((width, wide), 0) == ((i + j) & (occ - 1)) * occ + i)
-    first, second = jnp.zeros((1, wide), F32), jnp.zeros((1, wide), F32)
-    for k in range(occ):
-        first += jnp.where(i == k, occ_ref[k], 0.0)
-        second += jnp.where(j == k, occ_ref[k], 0.0)
-    total = dot(pieces[1], turned) + dot(pieces[0], turned)
-    out_ref[...] = total / (pair_of[:, :1] - (first + second))
+        turned_q[...] = unsort(width // wide - 1, wide, width, occ)
+        number = iota((1, width), 1)
+        i, j = number // occ, number & (occ - 1)
+        first, second = jnp.zeros((1, width), F32), jnp.zeros((1, width), F32)
+        for k in range(occ):
+            first += jnp.where(i == k, occ_ref[k], 0.0)
+            second += jnp.where(j == k, occ_ref[k], 0.0)
+        energy[...] = first + second
+
+    value = last_ref[...]
+    high = value.astype(BF16)
+    low = (value - high.astype(F32)).astype(BF16)
+    same = iota((lines, lines), 0) == iota((lines, lines), 1)
+    pair_of = jnp.sum(jnp.where(same, pair_ref[...], 0.0), axis=1, keepdims=True)
+    total = sum_ref[...] + (dot(low, turned_q[...]) + dot(high, turned_q[...]))
+    out_ref[...] = total / (pair_of - energy[...])
 
 
 def body(integrals, tile_count, tile_list, amplitudes, pair_energy, occ_energy, partner):
@@ -448,11 +466,11 @@
     anywhere = pl.BlockSpec(memory_space=pl.ANY)
     scalars = pl.BlockSpec(memory_space=pltpu.SMEM)
     vector = pl.BlockSpec(memory_space=pltpu.VMEM)
-    chosen = pl.pallas_call(
+    total, last = pl.pallas_call(
         functools.partial(ladder_kernel, n, ranks, occ),
-        out_shape=jax.ShapeDtypeStruct((rows, width), F32),
+        out_shape=[jax.ShapeDtypeStruct((rows, width), F32), jax.ShapeDtypeStruct((rows, WIDE), F32)],
         in_specs=[scalars, scalars, vector, anywhere, anywhere],
-        out_specs=vector,
+        out_specs=[vector, vector],
         scratch_shapes=[
             pltpu.VMEM((slots + 1, tile, tile), BF16),
             pltpu.VMEM((bc, share, width), BF16),
@@ -472,6 +490,7 @@
             pltpu.VMEM((rows, rows - own), BF16),
             pltpu.VMEM((2, own + 2 * half, WIDE), BF16),
             pltpu.VMEM((rows, WIDE), F32),
+            pltpu.VMEM((parts - 1, WIDE, width), BF16),
             *([pltpu.VMEM((units, own_p, WIDE), I16), pltpu.VMEM((units, -(-own_p // 128), 128), F32)] * 2),
             *([pltpu.VMEM((units, half, WIDE), I16), pltpu.VMEM((units, 1, 128), F32)] * 2),
             dma((4,)), dma, dma, dma((parts, ranks)), dma, dma((n,)),
@@ -483,16 +502,21 @@
         name="ladder",
     )(tile_list.reshape(slots), tile_count.reshape(1), partner[None, :], integrals, amplitudes)
 
-    whole = lambda k: (0, 0)
+    lines = max(rows // 4, 128)
     return pl.pallas_call(
         functools.partial(finish_kernel, occ),
-        grid=(parts,),
-        in_specs=[scalars, pl.BlockSpec((1, rows), whole), pl.BlockSpec((rows, width), whole)],
-        out_specs=pl.BlockSpec((rows, WIDE), lambda k: (0, k)),
+        grid=(rows // lines,),
+        in_specs=[
+            scalars,
+            pl.BlockSpec((1, lines), lambda k: (0, k)),
+            pl.BlockSpec((lines, width), lambda k: (k, 0)),
+            pl.BlockSpec((lines, WIDE), lambda k: (k, 0)),
+        ],
+        out_specs=pl.BlockSpec((lines, width), lambda k: (k, 0)),
         out_shape=jax.ShapeDtypeStruct((rows, width), F32),
-        scratch_shapes=[pltpu.VMEM((2, rows, width), BF16), pltpu.VMEM((rows, 128), F32)],
+        scratch_shapes=[pltpu.VMEM((WIDE, width), BF16), pltpu.VMEM((1, width), F32)],
         name="finish",
-    )(occ_energy, pair_energy[None, :], chosen)
+    )(occ_energy, pair_energy[None, :], total, last)
 
 
 def solution(mesh):

time: 102 us -> 101 us (level)
    pallas_call x1, Pallas kernels: 6.04 us -> 4.69 us  [body(): pl.pallas_call(functools.partial(finish_kernel, occ), grid=(rows // lines...]
where the time goes in v3:
time: 101 us
  Pallas kernels  100 us (99%)
    pallas_call x1, Pallas kernels, body(): pl.pallas_call(functools.partial(ladder_kernel, n, ranks, occ), out_shape...  95.3 us
    pallas_call x1, Pallas kernels, body(): pl.pallas_call(functools.partial(finish_kernel, occ), grid=(rows // lines...  4.69 us

profile of v3, /device:TPU:0, one launch (start us, length us, event | category | flops | bytes accessed | tf_op | source)
XLA Modules:
  0.0 100.6 jit_solution(7202453178045223659)
XLA Ops:
  0.7 95.3 %ladder.1 = (f32[512,1024]{1,0:T(8,128)}, f32[512,256]{1,0:T(8,128)}) custom-call(s32[32]{0:T(128)} %bitcast.7, s32[1]{0:T(128)} %bitcast.4.count_ref, s32[1,512]{1,0:T(1,128)} %bitcast.5, bf16[1,1,32,512,512]{4,3,2,1,0:T(8,128)(2,1)} %integrals.1, bf16[4,128,1024]{2,1,0:T(8,128)(2,1)} %amps.1), custom_call_target="tpu_custom_call" | custom-call | tf_op jit(solution)/shard_map/ladder/pallas_call | solution.py:469
  95.9 4.7 %finish.1 = f32[512,1024]{1,0:T(8,128)} custom-call(f32[32]{0:T(128)} %occ_ref.1, f32[1,512]{1,0:T(1,128)} %bitcast.6, f32[512,1024]{1,0:T(8,128)} %get-tuple-element.7.sum_ref, f32[512,256]{1,0:T(8,128)} %get-tuple-element.8.last_ref), custom_call_target="tpu_custom_call" | custom-call | tf_op jit(solution)/shard_map/finish/pallas_call | solution.py:506
